TPU v7x, 32 devices: a whole 2x2x4 slice. The times are simulated.
32 devices in a mesh: seq: 8 (over z, x), stream: 4 (over y, core).
Axes of the slice: x: 2, y: 2, z: 4, core: 2. Of those that a mesh axis runs over, the one named last changes fastest.
Arguments:
- tokens: bfloat16 [4, 4096, 768], P('stream', 'seq'), may hold values from -6 to 6
- segment_ids: int32 [4, 4096], P('stream', 'seq'), may hold values from -1 to 32, as said below
- query_key_value_weight: bfloat16 [768, 2304], replicated, may hold values from -0.21875 to 0.21875
- conv_kernel: bfloat16 [3, 2304], replicated, may hold values from -3 to 3
- attention_output_weight: bfloat16 [768, 768], replicated, may hold values from -0.875 to 0.875
- up_weight: bfloat16 [768, 3072], replicated, may hold values from -0.21875 to 0.21875
- down_weight: bfloat16 [3072, 768], replicated, may hold values from -0.109375 to 0.109375
- gain_attn: bfloat16 [768], replicated, may hold values from 0.5 to 1.5
- shift_attn: bfloat16 [768], replicated, may hold values from -3 to 3
- gain_ffn: bfloat16 [768], replicated, may hold values from 0.5 to 1.5
- shift_ffn: bfloat16 [768], replicated, may hold values from -3 to 3
- cotangent: bfloat16 [4, 4096, 768], P('stream', 'seq'), may hold values from -6 to 6
Outputs:
- out_tokens: bfloat16 [4, 4096, 768], P('stream', 'seq')
- grad_tokens: float32 [4, 4096, 768], P('stream', 'seq')
- grad_w_qkv: float32 [768, 2304], replicated
- grad_conv_kernel: float32 [3, 2304], replicated
- grad_w_out: float32 [768, 768], replicated
- grad_w_up: float32 [768, 3072], replicated
- grad_w_down: float32 [3072, 768], replicated
- grad_gain_attn: float32 [768], replicated
- grad_shift_attn: float32 [768], replicated
- grad_gain_ffn: float32 [768], replicated
- grad_shift_ffn: float32 [768], replicated
Inputs may be any that keep to these rules, and one draw needn't show every extreme that they name: `segment_ids`: along each pack the document numbers never fall and differ between documents; each document fills 128 to 256 consecutive slots, one of 256 slots in every pack; the last document of every pack has the number 4096 // 128; slots between documents hold -1, and so does the last slot of each pack.
All inputs are finite; a program needn't handle non-finite values.
Results may differ from a plain program's by a relative error of at most 0.019.
Values may be sent and summed in bfloat16 or wider, within the bound.
No kernel may reach another device: no remote copies, remote signals or barrier semaphores. Data moves between devices by JAX's collectives and lax.ppermute only.
A program may use at most 256 MiB of HBM per device.

v0:
```python
import math

import jax
import jax.numpy as jnp
from jax import lax
from jax.sharding import PartitionSpec as P

H = 12
HD = 64


EPSILON = 1e-05
MASKED = -1e30


def passed_along(block, axis, distance):
    devices = range(lax.axis_size(axis))
    route = [(i - distance, i) for i in devices if i - distance in devices]
    return lax.ppermute(block, axis, route)


def layer_norm(field, gain, shift):
    center = field - jnp.mean(field, -1, keepdims=True)
    spread = jnp.mean(center * center, -1, keepdims=True)
    return center * lax.rsqrt(spread + EPSILON) * gain + shift


def square_relu(field):
    return jnp.square(jnp.maximum(field, 0.0))


def conv_local(extended, kernel, same_one, same_two):
    row_count = extended.shape[1] - 2
    result = kernel[0] * extended[:, 2:]
    result = result + kernel[1] * extended[:, 1 : row_count + 1] * same_one
    result = result + kernel[2] * extended[:, :row_count] * same_two
    return result


def pair_scores(queries, key_rows, query_ids, key_ids, query_pos, key_pos):
    raw_scores = jnp.einsum(
        "sqhd,skhd->shqk", queries, key_rows, preferred_element_type=jnp.float32
    )
    allowed = (query_ids[:, :, None] == key_ids[:, None, :]) & (key_ids[:, None, :] >= 0)
    allowed = (
        allowed
        & (key_pos[None, None, :] <= query_pos[None, :, None])
        & (key_pos[None, None, :] >= 0)
    )
    allowed = allowed | (key_pos[None, None, :] == query_pos[None, :, None])
    return jnp.where(allowed[:, None], raw_scores * (1.0 / math.sqrt(HD)), MASKED)


def on_device(
    tokens,
    segment_ids,
    query_key_value_weight,
    conv_kernel,
    attention_output_weight,
    up_weight,
    down_weight,
    gain_attn,
    shift_attn,
    gain_ffn,
    shift_ffn,
    cotangent,
):
    pack_count, slot_count, model_width = tokens.shape
    device_at = lax.axis_index("seq")
    slot_steps = jnp.arange(slot_count, dtype=jnp.int32)
    query_pos = device_at * slot_count + slot_steps
    own_live = segment_ids >= 0
    active_token_mask = own_live.astype(jnp.float32)[..., None]
    inputs = tokens.astype(jnp.float32)
    normalized_first, norm_one_back = jax.vjp(
        layer_norm, inputs, gain_attn.astype(jnp.float32), shift_attn.astype(jnp.float32)
    )
    normalized_first_narrow = normalized_first.astype(jnp.bfloat16)
    mixed_query_key_value = jnp.einsum(
        "jmc,ct->jmt",
        normalized_first_narrow,
        query_key_value_weight,
        preferred_element_type=jnp.float32,
    )
    halo_rows, halo_ids = passed_along(
        (mixed_query_key_value[:, -2:], segment_ids[:, -2:]), "seq", 1
    )
    extended = jnp.concatenate([halo_rows, mixed_query_key_value], 1)
    extended_ids = jnp.concatenate([halo_ids, segment_ids], 1)
    same_one = ((extended_ids[:, 1 : slot_count + 1] == segment_ids) & own_live).astype(
        jnp.float32
    )[..., None]
    same_two = ((extended_ids[:, :slot_count] == segment_ids) & own_live).astype(jnp.float32)[
        ..., None
    ]
    convolved, conv_back = jax.vjp(
        lambda field, weights: conv_local(field, weights, same_one, same_two),
        extended,
        conv_kernel.astype(jnp.float32),
    )
    conv_low = convolved.astype(jnp.bfloat16)
    head_shape = (pack_count, slot_count, H, HD)
    queries = conv_low[..., :model_width].reshape(head_shape)
    pair_kv = conv_low[..., model_width:]
    prior_kv, prior_ids = passed_along((pair_kv, segment_ids), "seq", 1)
    shard_kv = jnp.stack([prior_kv, pair_kv])
    shard_ids = jnp.stack([prior_ids, segment_ids])
    shard_at = device_at - 1 + jnp.arange(2, dtype=jnp.int32)
    shard_total = shard_kv.shape[0]
    first_id = jnp.min(jnp.where(own_live, segment_ids, 1 << 30))

    def shard_view(shard):
        block_kv = lax.dynamic_index_in_dim(shard_kv, shard, 0, keepdims=False)
        key_rows = block_kv[..., :model_width].reshape(head_shape)
        value_rows = block_kv[..., model_width:].reshape(head_shape)
        key_ids = lax.dynamic_index_in_dim(shard_ids, shard, 0, keepdims=False)
        owner = lax.dynamic_index_in_dim(shard_at, shard, 0, keepdims=False)
        key_pos = owner * slot_count + slot_steps
        useful = (owner == device_at) | (owner < device_at) & (owner >= 0) & (
            jnp.max(key_ids) >= first_id
        )
        return (key_rows, value_rows, key_ids, key_pos, useful)

    def keep_state(state):
        return state

    def top_step(shard, state):
        key_rows, value_rows, key_ids, key_pos, useful = shard_view(shard)

        def top_work(inner):
            row_top, row_total = inner
            scores = pair_scores(queries, key_rows, segment_ids, key_ids, query_pos, key_pos)
            new_top = jnp.maximum(row_top, jnp.max(scores, -1))
            row_total = row_total * jnp.exp(row_top - new_top) + jnp.sum(
                jnp.exp(scores - new_top[..., None]), -1
            )
            return (new_top, row_total)

        return lax.cond(useful, top_work, keep_state, state)

    stat_shape = (pack_count, H, slot_count)
    row_top, row_total = lax.fori_loop(
        0,
        shard_total,
        top_step,
        (jnp.full(stat_shape, MASKED, jnp.float32), jnp.zeros(stat_shape, jnp.float32)),
    )
    log_total = row_top + jnp.log(row_total)

    def probs_for(key_rows, key_ids, key_pos):
        scores = pair_scores(queries, key_rows, segment_ids, key_ids, query_pos, key_pos)
        return jnp.exp(scores - log_total[..., None])

    def out_step(shard, state):
        key_rows, value_rows, key_ids, key_pos, useful = shard_view(shard)

        def out_work(inner):
            probs = probs_for(key_rows, key_ids, key_pos)
            return inner + jnp.einsum(
                "shqk,skhd->sqhd",
                probs.astype(jnp.bfloat16),
                value_rows,
                preferred_element_type=jnp.float32,
            )

        return lax.cond(useful, out_work, keep_state, state)

    attention_result = lax.fori_loop(0, shard_total, out_step, jnp.zeros(head_shape, jnp.float32))
    attention_result = attention_result.reshape(pack_count, slot_count, model_width).astype(
        jnp.bfloat16
    )
    residual_branch = jnp.einsum(
        "jmc,ct->jmt", attention_result, attention_output_weight, preferred_element_type=jnp.float32
    )
    middle_state = inputs + active_token_mask * residual_branch
    normalized_second, norm_two_back = jax.vjp(
        layer_norm, middle_state, gain_ffn.astype(jnp.float32), shift_ffn.astype(jnp.float32)
    )
    normalized_second_narrow = normalized_second.astype(jnp.bfloat16)
    hidden_state = jnp.einsum(
        "zha,ay->zhy", normalized_second_narrow, up_weight, preferred_element_type=jnp.float32
    )
    activated_hidden, relu_back = jax.vjp(square_relu, hidden_state)
    activated_narrow = activated_hidden.astype(jnp.bfloat16)
    feedforward_output = jnp.einsum(
        "nxg,gi->nxi", activated_narrow, down_weight, preferred_element_type=jnp.float32
    )
    out_tokens = (middle_state + active_token_mask * feedforward_output).astype(jnp.bfloat16)
    grad_out = cotangent.astype(jnp.float32)
    gradient_residual_branch = (active_token_mask * grad_out).astype(jnp.bfloat16)
    grad_w_down = jnp.einsum(
        "ipr,iph->rh",
        activated_narrow,
        gradient_residual_branch,
        preferred_element_type=jnp.float32,
    )
    gradient_activated = jnp.einsum(
        "owr,ar->owa", gradient_residual_branch, down_weight, preferred_element_type=jnp.float32
    )
    gradient_hidden_state = relu_back(gradient_activated)[0].astype(jnp.bfloat16)
    grad_w_up = jnp.einsum(
        "jtw,jth->wh",
        normalized_second_narrow,
        gradient_hidden_state,
        preferred_element_type=jnp.float32,
    )
    grad_normed_two = jnp.einsum(
        "ytw,pw->ytp", gradient_hidden_state, up_weight, preferred_element_type=jnp.float32
    )
    grad_middle_part, grad_gain_ffn, grad_shift_ffn = norm_two_back(grad_normed_two)
    grad_middle = grad_out + grad_middle_part
    gradient_attention_branch = (active_token_mask * grad_middle).astype(jnp.bfloat16)
    grad_w_out = jnp.einsum(
        "tir,tiv->rv",
        attention_result,
        gradient_attention_branch,
        preferred_element_type=jnp.float32,
    )
    grad_heads = (
        jnp.einsum(
            "tig,ag->tia",
            gradient_attention_branch,
            attention_output_weight,
            preferred_element_type=jnp.float32,
        )
        .astype(jnp.bfloat16)
        .reshape(head_shape)
    )

    def delta_step(shard, state):
        key_rows, value_rows, key_ids, key_pos, useful = shard_view(shard)

        def delta_work(inner):
            probs = probs_for(key_rows, key_ids, key_pos)
            grad_probs = jnp.einsum(
                "sqhd,skhd->shqk", grad_heads, value_rows, preferred_element_type=jnp.float32
            )
            return inner + jnp.sum(probs * grad_probs, -1)

        return lax.cond(useful, delta_work, keep_state, state)

    row_delta = lax.fori_loop(0, shard_total, delta_step, jnp.zeros(stat_shape, jnp.float32))

    def grad_step(shard, state):
        key_rows, value_rows, key_ids, key_pos, useful = shard_view(shard)

        def grad_work(inner):
            grad_queries, key_terms = inner
            probs = probs_for(key_rows, key_ids, key_pos)
            grad_probs = jnp.einsum(
                "sqhd,skhd->shqk", grad_heads, value_rows, preferred_element_type=jnp.float32
            )
            grad_scores = (
                probs * (grad_probs - row_delta[..., None]) * (1.0 / math.sqrt(HD))
            ).astype(jnp.bfloat16)
            grad_queries = grad_queries + jnp.einsum(
                "shqk,skhd->sqhd", grad_scores, key_rows, preferred_element_type=jnp.float32
            )
            grad_keys = jnp.einsum(
                "shqk,sqhd->skhd", grad_scores, queries, preferred_element_type=jnp.float32
            )
            grad_values = jnp.einsum(
                "shqk,sqhd->skhd",
                probs.astype(jnp.bfloat16),
                grad_heads,
                preferred_element_type=jnp.float32,
            )
            key_piece = jnp.concatenate(
                [
                    grad_keys.reshape(pack_count, slot_count, model_width),
                    grad_values.reshape(pack_count, slot_count, model_width),
                ],
                -1,
            )
            key_terms = lax.dynamic_update_index_in_dim(key_terms, key_piece, shard, 0)
            return (grad_queries, key_terms)

        return lax.cond(useful, grad_work, keep_state, state)

    term_init = jnp.zeros((shard_total, pack_count, slot_count, 2 * model_width), jnp.float32)
    grad_queries, key_terms = lax.fori_loop(
        0, shard_total, grad_step, (jnp.zeros(head_shape, jnp.float32), term_init)
    )
    grad_kv = key_terms[1] + passed_along(key_terms[0].astype(jnp.bfloat16), "seq", -1).astype(
        jnp.float32
    )
    grad_conv = jnp.concatenate(
        [grad_queries.reshape(pack_count, slot_count, model_width), grad_kv], -1
    )
    grad_extended, grad_kernel = conv_back(grad_conv)
    back_rows = passed_along(grad_extended[:, :2], "seq", -1)
    gradient_mixed_projection = grad_extended[:, 2:]
    gradient_mixed_projection = jnp.concatenate(
        [gradient_mixed_projection[:, :-2], gradient_mixed_projection[:, -2:] + back_rows], 1
    ).astype(jnp.bfloat16)
    grad_w_qkv = jnp.einsum(
        "tir,tiv->rv",
        normalized_first_narrow,
        gradient_mixed_projection,
        preferred_element_type=jnp.float32,
    )
    gradient_normalized_first = jnp.einsum(
        "tig,ag->tia",
        gradient_mixed_projection,
        query_key_value_weight,
        preferred_element_type=jnp.float32,
    )
    grad_input_part, grad_gain_attn, grad_shift_attn = norm_one_back(gradient_normalized_first)
    grad_tokens = grad_middle + grad_input_part
    grads = [
        grad_w_qkv,
        grad_kernel,
        grad_w_out,
        grad_w_up,
        grad_w_down,
        grad_gain_attn,
        grad_shift_attn,
        grad_gain_ffn,
        grad_shift_ffn,
    ]
    flat = jnp.concatenate([piece.reshape(-1) for piece in grads])
    shares = lax.psum_scatter(
        flat.astype(jnp.bfloat16), "seq", scatter_dimension=0, tiled=True
    ).astype(jnp.float32)
    shares = lax.psum(shares.astype(jnp.bfloat16), "stream").astype(jnp.float32)
    summed = lax.all_gather(shares.astype(jnp.bfloat16), "seq", axis=0, tiled=True).astype(
        shares.dtype
    )
    results = []
    offset = 0
    for piece in grads:
        count = piece.size
        results.append(summed[offset : offset + count].reshape(piece.shape))
        offset = offset + count
    return (
        out_tokens,
        grad_tokens,
        results[0],
        results[1],
        results[2],
        results[3],
        results[4],
        results[5],
        results[6],
        results[7],
        results[8],
    )


def solution(mesh):
    return jax.shard_map(
        on_device,
        mesh=mesh,
        in_specs=(
            P("stream", "seq", None),
            P("stream", "seq"),
            P(),
            P(),
            P(),
            P(),
            P(),
            P(),
            P(),
            P(),
            P(),
            P("stream", "seq", None),
        ),
        out_specs=(
            P("stream", "seq", None),
            P("stream", "seq", None),
            P(),
            P(),
            P(),
            P(),
            P(),
            P(),
            P(),
            P(),
            P(),
        ),
        check_vma=False,
    )
```

profile of v0, /device:TPU:0, one launch (start us, length us, event | category | flops | bytes accessed | tf_op | source)
XLA Modules:
  0.0 1588.4 jit_solution(7274010136364462006)
XLA Ops:
  41.8 25.5 %collective-permute-done = s32[1,512]{1,0:T(1,128)S(1)} collective-permute-done((s32[1,512]{1,0:T(1,128)S(1)}, s32[1,512]{1,0:T(1,128)S(1)}, u32[]{:S(2)}, u32[]{:S(2)}) %collective-permute-start) | collective-permute-done | bytes 2080 | tf_op jit(solution)/shard_map/ppermute | solution.py:19
  81.4 21.0 %while.66 = (s32[]{:T(128)}, f32[1,12,512]{2,1,0:T(8,128)}, f32[1,12,512]{2,1,0:T(8,128)}, s32[2]{0:T(128)}, s32[]{:T(128)}, /*index=5*/s32[2,1,512]{2,1,0:T(1,1...) while((s32[]{:T(128)}, f32[1,12,512]{2,1,0:T(8,128)}, ...), condition=%wide.region_9.10_spmd.clone, body=%wide.region_3.9_spmd.clone.sunk | while | flops 426523136 | bytes 36882872 | solution.py:142
  91.6 10.8 conditional.12
  105.1 23.4 %while.67 = (s32[]{:T(128)}, f32[1,512,12,64]{1,3,2,0:T(8,128)}, s32[2]{0:T(128)}, s32[]{:T(128)}, s32[2,1,512]{2,1,0:T(1,128)S(1)}, /*index=5*/s32[]{:T(128)}, ...) while((s32[]{:T(128)}, f32[1,512,12,64]{1,3,2,0:T(8,128)}, ...), condition=%wide.region_14.15_spmd.clone, body=%wide.region_10.14_spmd.clone.sunk | while | flops 820120064 | bytes 12372291 | solution.py:168
  115.8 12.2 conditional.13
  150.8 21.0 %while.68 = (s32[]{:T(128)}, f32[1,12,512]{2,1,0:T(8,128)}, s32[2]{0:T(128)}, s32[]{:T(128)}, s32[2,1,512]{2,1,0:T(1,128)S(1)}, /*index=5*/s32[]{:T(128)}, s32[1...) while((s32[]{:T(128)}, f32[1,12,512]{2,1,0:T(8,128)}, ...), condition=%wide.region_24.25_spmd.clone, body=%wide.region_19.24_spmd.clone.sunk | while | flops 822872576 | bytes 41666984 | solution.py:242
  161.2 10.5 conditional.14
  176.6 41.2 %while.69 = (s32[]{:T(128)}, f32[1,512,12,64]{1,3,2,0:T(8,128)}, f32[2,1,512,1536]{2,3,1,0:T(8,128)}, s32[2]{0:T(128)}, s32[]{:T(128)}, /*index=5*/s32[2,1,512]{...) while((s32[]{:T(128)}, f32[1,512,12,64]{1,3,2,0:T(8,128)}, ...), condition=%wide.region_29.30_spmd.clone, body=%wide.region_25.29_spmd.clone.sunk | while | flops 2050886144 | bytes 144902832 | solution.py:281
  187.7 30.1 %conditional.15 = ((f32[1,512,12,64]{1,3,2,0:T(8,128)}, f32[2,1,512,1536]{2,3,1,0:T(8,128)})) conditional(s32[]{:T(128)} %convert_element_type.256, (f32[1,512,12,64]{1,3,2,0:T(8,128)}, f32[2,1,512,1536]{2,3,1,0:T(8,128)}) %tuple.244, (bf16[2,1,512,1536]{2,3,1,0:T(8,128)(2,1)}, s32[]{:T(128)}, s32[1,512]{1,0:T(1,128)S(1)}, ...), branch_computations={%region_27.27_spmd, %region_28.28_spmd} | conditional | flops 2050885632 | bytes 144896320 | solution.py:278
  228.9 7.9 convolution_convert_fusion
  236.7 9.4 reshape.1646
  296.7 61.5 %collective-permute-done.5 = f32[1,2,2304]{2,1,0:T(2,128)} collective-permute-done((f32[1,2,2304]{2,1,0:T(2,128)}, f32[1,2,2304]{2,1,0:T(2,128)}, u32[]{:S(2)}, u32[]{:S(2)}) %collective-permute-start.5) | collective-permute-done | bytes 18464 | tf_op jit(solution)/shard_map/ppermute | solution.py:19
  384.8 19.2 %dynamic-update-slice.3 = bf16[7087872]{0:T(1024)(128)(2,1)} dynamic-update-slice(bf16[7087872]{0:T(1024)(128)(2,1)} %dynamic-update-slice.2, bf16[589824]{0:T(1024)(128)(2,1)} %reshape.1644, s32[]{} %constant.348) | dynamic-update-slice | bytes 2359300
  404.0 72.5 %dynamic-update-slice.4 = bf16[7087872]{0:T(1024)(128)(2,1)} dynamic-update-slice(bf16[7087872]{0:T(1024)(128)(2,1)} %dynamic-update-slice.3, bf16[2359296]{0:T(1024)(128)(2,1)} %bitcast.265, s32[]{} %constant.349) | dynamic-update-slice | bytes 9437188
  476.5 72.4 %dynamic-update-slice.5 = bf16[7087872]{0:T(1024)(128)(2,1)} dynamic-update-slice(bf16[7087872]{0:T(1024)(128)(2,1)} %dynamic-update-slice.4, bf16[2359296]{0:T(1024)(128)(2,1)} %reshape.1646, s32[]{} %constant.350) | dynamic-update-slice | bytes 9437188
  555.5 448.2 %all-reduce.16.cloned.1.call-done = bf16[7087872]{0:T(1024)(128)(2,1)} async-done(((bf16[7087872]{0:T(1024)(128)(2,1)}), bf16[7087872]{0:T(1024)(128)(2,1)}) %all-reduce.16.cloned.1.call-update) | async-done | bytes 14175760
  1008.2 44.8 %all-reduce.12.cloned.1.call-done = bf16[885984]{0:T(1024)(128)(2,1)} async-done(((bf16[885984]{0:T(1024)(128)(2,1)}), bf16[885984]{0:T(1024)(128)(2,1)}) %all-reduce.12.cloned.1.call-update) | async-done | bytes 1771984 | tf_op jit(solution)/shard_map/psum | solution.py:325
  1058.2 28.2 %dynamic-update-slice = bf16[7087872]{0:T(1024)(128)(2,1)} dynamic-update-slice(bf16[7087872]{0:T(1024)(128)(2,1)} %broadcast.947, bf16[885984]{0:T(1024)(128)(2,1)} %all-reduce.12.cloned.1.call-done, u32[]{:T(128)} %bitcast.83) | dynamic-update-slice | bytes 3543940
  1087.0 8.4 fusion.78
  1097.4 428.8 %all-reduce.14.cloned.1.call-done = bf16[7087872]{0:T(1024)(128)(2,1)} async-done(((bf16[7087872]{0:T(1024)(128)(2,1)}), bf16[7087872]{0:T(1024)(128)(2,1)}) %all-reduce.14.cloned.1.call-update) | async-done | bytes 14175760
  1539.9 8.2 reshape.1647
  1548.1 10.0 fusion.112
  1558.1 11.3 slice.198
  1569.4 10.9 reshape.1649
  (362 shorter events, 274.8 us)
Async XLA Ops:
  7.2 996.5 %all-reduce.16.cloned.1.call-start = ((), (), s32[]{:S(2)}) async-start(), calls=%async_computation.2 | async-start | bytes 28352512
  8.1 16.2 %collective-permute-start.2 = (s32[1,2]{1,0:T(1,128)S(1)}, s32[1,2]{1,0:T(1,128)S(1)}, u32[]{:S(2)}, u32[]{:S(2)}) collective-permute-start(s32[1,2]{1,0:T(1,128)S(1)} %slice.180), channel_id=1, source_target_pairs={{0,4},{4,8},{8,12},{12,16},{16,20},{20,24},{24,28},{1,5},{5,9},{9,... | collective-permute-start | bytes 32 | tf_op jit(solution)/shard_map/ppermute | solution.py:19
  20.7 4.9 collective-permute-start.1
  28.1 12.5 copy-start.80
  28.1 13.1 copy-start.81
  30.6 41.1 %collective-permute-start.3 = (bf16[1,512,1536]{2,1,0:T(8,128)(2,1)}, bf16[1,512,1536]{2,1,0:T(8,128)(2,1)}, u32[]{:S(2)}, u32[]{:S(2)}) collective-permute-start(bf16[1,512,1536]{2,1,0:T(8,128)(2,1)} %get-tuple-element.1763), channel_id=1, source_target_pairs={{0,4},{4,8},{8,12},{12,16},{16,20},{20,24},{24,28},{1,5},{5,9},{9,... | collective-permute-start | bytes 4718600 | tf_op jit(solution)/shard_map/ppermute | solution.py:19
  35.9 31.4 %collective-permute-start = (s32[1,512]{1,0:T(1,128)S(1)}, s32[1,512]{1,0:T(1,128)S(1)}, u32[]{:S(2)}, u32[]{:S(2)}) collective-permute-start(s32[1,512]{1,0:T(1,128)S(1)} %copy-done.27), channel_id=1, source_target_pairs={{0,4},{4,8},{8,12},{12,16},{16,20},{20,24},{24,28},{1,5},{5,9},{9,... | collective-permute-start | bytes 6152 | tf_op jit(solution)/shard_map/ppermute | solution.py:19
  217.8 11.1 copy-start.68
  227.6 40.8 %collective-permute-start.4 = (bf16[1,512,1536]{2,1,0:T(8,128)(2,1)}, bf16[1,512,1536]{2,1,0:T(8,128)(2,1)}, u32[]{:S(2)}, u32[]{:S(2)}) collective-permute-start(bf16[1,512,1536]{2,1,0:T(8,128)(2,1)} %fusion.75), channel_id=1, source_target_pairs={{4,0},{8,4},{12,8},{16,12},{20,16},{24,20},{28,24},{5,1},{9,5},{13... | collective-permute-start | bytes 4718600 | tf_op jit(solution)/shard_map/ppermute | solution.py:19
  236.7 11.5 copy-start.57
  236.7 11.5 copy-start.66
  236.7 11.5 copy-start.71
  236.7 11.5 copy-start.79
  291.6 66.6 %collective-permute-start.5 = (f32[1,2,2304]{2,1,0:T(2,128)}, f32[1,2,2304]{2,1,0:T(2,128)}, u32[]{:S(2)}, u32[]{:S(2)}) collective-permute-start(f32[1,2,2304]{2,1,0:T(2,128)} %pad_add_fusion.1), channel_id=1, source_target_pairs={{4,0},{8,4},{12,8},{16,12},{20,16},{24,20},{28,24},{5,1},{9,5},{13... | collective-permute-start | bytes 55304 | tf_op jit(solution)/shard_map/ppermute | solution.py:19
  296.7 62.5 %copy-start.16 = (bf16[1,512,768]{2,1,0:T(8,128)(2,1)S(1)}, bf16[1,512,768]{2,1,0:T(8,128)(2,1)}, u32[]{:S(2)}) copy-start(bf16[1,512,768]{2,1,0:T(8,128)(2,1)} %param.28) | copy-start | bytes 2359300
  296.7 62.5 %copy-start.26 = (bf16[510,2304]{1,0:T(8,128)(2,1)S(1)}, bf16[510,2304]{1,0:T(8,128)(2,1)}, u32[]{:S(2)}) copy-start(bf16[510,2304]{1,0:T(8,128)(2,1)} %fusion.65) | copy-start | bytes 7050244
  296.7 62.5 %copy-start.43 = (f32[768]{0:T(1024)S(1)}, f32[768]{0:T(1024)}, u32[]{:S(2)}) copy-start(f32[768]{0:T(1024)} %copy-done.42) | copy-start | bytes 9220
  296.7 62.5 %copy-start.46 = (f32[512]{0:T(512)S(1)}, f32[512]{0:T(512)}, u32[]{:S(2)}) copy-start(f32[512]{0:T(512)} %copy-done.45) | copy-start | bytes 6148
  476.5 72.4 %copy-start.75 = (bf16[768]{0:T(1024)(128)(2,1)S(1)}, bf16[768]{0:T(1024)(128)(2,1)}, u32[]{:S(2)}) copy-start(bf16[768]{0:T(1024)(128)(2,1)} %get-tuple-element.1627) | copy-start | bytes 4612
  476.5 73.8 %copy-start.74 = (bf16[768]{0:T(1024)(128)(2,1)S(1)}, bf16[768]{0:T(1024)(128)(2,1)}, u32[]{:S(2)}) copy-start(bf16[768]{0:T(1024)(128)(2,1)} %reduce_sum.178) | copy-start | bytes 4612
  476.5 75.2 %copy-start.83 = (bf16[768]{0:T(1024)(128)(2,1)S(1)}, bf16[768]{0:T(1024)(128)(2,1)}, u32[]{:S(2)}) copy-start(bf16[768]{0:T(1024)(128)(2,1)} %get-tuple-element.1625) | copy-start | bytes 4612
  476.5 76.5 %copy-start.72 = (bf16[768]{0:T(1024)(128)(2,1)S(1)}, bf16[768]{0:T(1024)(128)(2,1)}, u32[]{:S(2)}) copy-start(bf16[768]{0:T(1024)(128)(2,1)} %reduce_sum.183) | copy-start | bytes 4612
  553.6 499.4 %all-reduce.12.cloned.1.call-start = ((), (), s32[]{:S(2)}) async-start(), calls=%async_computation | async-start | bytes 3547136 | tf_op jit(solution)/shard_map/psum | solution.py:325
  1007.3 518.9 %all-reduce.14.cloned.1.call-start = ((), (), s32[]{:S(2)}) async-start(), calls=%async_computation.1 | async-start | bytes 28352512
  (79 other events, 346.1 us)
Sparse Core Ops, SparseCore 0:
  553.7 449.8 all-reduce.15
  1007.4 45.4 all-reduce.11
  1086.5 439.7 all-reduce.13
where the time goes:
time: 1620 us; the launch traced here: 1590 us
  waiting for transfers between devices  1010 us (62%)
  local copies, waits for them, and re-layouts  363 us (22%)
  matrix products  86.2 us (5%)
  other arithmetic  62.4 us (4%)
  loops' own time  30.1 us (2%)
  starting transfers between devices  20.5 us (1%)
  between operations  16.3 us (1%)
    unnamed x5, waiting for transfers between devices  877 us
    unnamed x174, local copies, waits for them, and re-layouts  228 us
    ppermute x6, waiting for transfers between devices, passed_along(): return lax.ppermute(block, axis, route)  87.7 us
    psum x1, waiting for transfers between devices, on_device(): shares = lax.psum(shares.astype(jnp.bfloat16), 'stream').astype(jnp.float32)  44.8 us
    slice x7, local copies, waits for them, and re-layouts, on_device(): results.append(summed[offset:offset + count].reshape(piece.shape))  34.9 us
  transfers between devices with their start and end apart: 9, of which 6 were waited for; matrix products, arithmetic and copies ran while one was open for 4% of the time, Pallas kernels for 0%

commit v1 on v0

--- a/solution.py
+++ b/solution.py
@@ -318,20 +318,21 @@
         grad_gain_ffn,
         grad_shift_ffn,
     ]
-    flat = jnp.concatenate([piece.reshape(-1) for piece in grads])
-    shares = lax.psum_scatter(
-        flat.astype(jnp.bfloat16), "seq", scatter_dimension=0, tiled=True
-    ).astype(jnp.float32)
-    shares = lax.psum(shares.astype(jnp.bfloat16), "stream").astype(jnp.float32)
-    summed = lax.all_gather(shares.astype(jnp.bfloat16), "seq", axis=0, tiled=True).astype(
-        shares.dtype
-    )
+    both = ("seq", "stream")
+    small = [grads[1].reshape(-1)] + grads[5:]
+    small_sum = lax.psum(jnp.concatenate(small), both)
+    big = {
+        at: lax.psum(grads[at].astype(jnp.bfloat16), both).astype(jnp.float32)
+        for at in (4, 3, 2, 0)
+    }
     results = []
     offset = 0
-    for piece in grads:
-        count = piece.size
-        results.append(summed[offset : offset + count].reshape(piece.shape))
-        offset = offset + count
+    for at, piece in enumerate(grads):
+        if at in big:
+            results.append(big[at])
+        else:
+            results.append(small_sum[offset : offset + piece.size].reshape(piece.shape))
+            offset = offset + piece.size
     return (
         out_tokens,
         grad_tokens,

time: 1620 us -> 633 us (0.39); the launches traced: 1590 us -> 626 us
  waiting for transfers between devices: 1010 us -> 266 us
  local copies, waits for them, and re-layouts: 363 us -> 82.5 us
  blocking collectives: 0 us -> 44.6 us
    unnamed x5 -> x1, waiting for transfers between devices: 877 us -> 0.02 us
    unnamed x174 -> x150, local copies, waits for them, and re-layouts: 228 us -> 18 us
    psum x1, waiting for transfers between devices: 44.8 us -> 159 us  [on_device(): lax.psum(grads[at].astype(jnp.bfloat16), both).astype(jnp.float32)]
    psum x0 -> x1, blocking collectives: none -> 44.6 us  [on_device(): small_sum = lax.psum(jnp.concatenate(small), both)]
    reshape x7 -> x2, local copies, waits for them, and re-layouts: 41.7 us -> 2.79 us  [the longest x1 1.39 us: on_device(): results.append(small_sum[offset:offset + piece.size].reshape(piece.shape))]
    slice x7 -> x2, local copies, waits for them, and re-layouts: 34.9 us -> 2.74 us  [on_device(): results.append(small_sum[offset:offset + piece.size].reshape(piece.shape))]
    ppermute x6, waiting for transfers between devices: 87.7 us -> 108 us  [passed_along(): return lax.ppermute(block, axis, route)]
    convert_element_type x0 -> x4, other arithmetic: none -> 16.6 us  [on_device(): lax.psum(grads[at].astype(jnp.bfloat16), both).astype(jnp.float32)]
  transfers between devices with their start and end apart: 9 -> 7, of which waited for: 6 -> 5; matrix products, arithmetic and copies ran while one was open for 4% -> 14% of each run, Pallas kernels for 0% -> 0%
where the time goes in v1:
time: 633 us; the launch traced here: 626 us
  waiting for transfers between devices  266 us (42%)
  matrix products  94 us (15%)
  local copies, waits for them, and re-layouts  82.5 us (13%)
  other arithmetic  75.2 us (12%)
  blocking collectives  44.6 us (7%)
  loops' own time  28.1 us (4%)
  starting transfers between devices  20.3 us (3%)
  between operations  15.2 us (2%)
    psum x1, waiting for transfers between devices, on_device(): lax.psum(grads[at].astype(jnp.bfloat16), both).astype(jnp.float32)  159 us
    ppermute x6, waiting for transfers between devices, passed_along(): return lax.ppermute(block, axis, route)  108 us
    psum x1, blocking collectives, on_device(): small_sum = lax.psum(jnp.concatenate(small), both)  44.6 us
    ppermute x6, starting transfers between devices, passed_along(): return lax.ppermute(block, axis, route)  20.3 us
    unnamed x150, local copies, waits for them, and re-layouts  18 us
    convert_element_type x4, other arithmetic, on_device(): lax.psum(grads[at].astype(jnp.bfloat16), both).astype(jnp.float32)  16.6 us
  transfers between devices with their start and end apart: 7, of which 5 were waited for; matrix products, arithmetic and copies ran while one was open for 14% of the time, Pallas kernels for 0%

profile of v1, /device:TPU:0, one launch (start us, length us, event | category | flops | bytes accessed | tf_op | source)
XLA Modules:
  0.0 626.4 jit_solution(17301279273125556064)
XLA Ops:
  8.1 5.0 collective-permute-start.2
  30.6 5.4 collective-permute-start.3
  42.0 25.3 %collective-permute-done = s32[1,512]{1,0:T(1,128)S(1)} collective-permute-done((s32[1,512]{1,0:T(1,128)S(1)}, s32[1,512]{1,0:T(1,128)S(1)}, u32[]{:S(2)}, u32[]{:S(2)}) %collective-permute-start) | collective-permute-done | bytes 2080 | tf_op jit(solution)/shard_map/ppermute | solution.py:19
  85.1 20.9 %while.66 = (s32[]{:T(128)}, f32[1,12,512]{2,1,0:T(8,128)}, f32[1,12,512]{2,1,0:T(8,128)}, s32[2]{0:T(128)}, s32[]{:T(128)}, /*index=5*/s32[2,1,512]{2,1,0:T(1,1...) while((s32[]{:T(128)}, f32[1,12,512]{2,1,0:T(8,128)}, ...), condition=%wide.region_9.10_spmd.clone, body=%wide.region_3.9_spmd.clone.sunk | while | flops 426523136 | bytes 36882872 | solution.py:142
  95.2 10.8 %conditional.12 = ((f32[1,12,512]{2,1,0:T(8,128)}, f32[1,12,512]{2,1,0:T(8,128)})) conditional(s32[]{:T(128)} %convert_element_type.280, (f32[1,12,512]{2,1,0:T(8,128)}, f32[1,12,512]{2,1,0:T(8,128)}) %tuple.228, (s32[1,512]{1,0:T(1,128)S(1)}, s32[1,1,512]{2,1,0:T(1,128)S(1)}, s32[]{:T(128)}, s32[512]{0:T(512)S(1)}, s32[]{:T(128)}, ...), branch_computations={%region_5.5_spmd, %region_6.8_spmd} | conditional | flops 426522624 | bytes 36876420 | solution.py:139
  108.7 23.4 %while.67 = (s32[]{:T(128)}, f32[1,512,12,64]{1,3,2,0:T(8,128)}, s32[2]{0:T(128)}, s32[]{:T(128)}, s32[2,1,512]{2,1,0:T(1,128)S(1)}, /*index=5*/s32[]{:T(128)}, ...) while((s32[]{:T(128)}, f32[1,512,12,64]{1,3,2,0:T(8,128)}, ...), condition=%wide.region_14.15_spmd.clone, body=%wide.region_10.14_spmd.clone.sunk | while | flops 820120064 | bytes 12372291 | solution.py:168
  118.8 13.1 %conditional.13 = (f32[1,512,12,64]{1,3,2,0:T(8,128)}) conditional(s32[]{:T(128)} %convert_element_type.281, f32[1,512,12,64]{1,3,2,0:T(8,128)} %get-tuple-element.2104, (bf16[2,1,512,1536]{2,3,1,0:T(8,128)(2,1)}, s32[]{:T(128)}, s32[1,512]{1,0:T(1,128)S(1)}, s32[1,1,512]{2,1,0:T(1,128)S(1)}, s32[]{:T(128)}, /*index=5*/s32[512]{0:T(512)S(1)}, ...), branch_computations={%region_12.12_spmd, %region_13.13_spmd} | conditional | flops 820119552 | bytes 12365856 | solution.py:166
  123.5 8.5 %bitcast_add_fusion.1 = f32[1,512,12,64]{1,3,2,0:T(8,128)} fusion(f32[1,512,12,64]{1,3,2,0:T(8,128)} %get-tuple-element.1249, bf16[512,12,64]{0,2,1:T(8,128)(2,1)} %bitcast.256, f32[12,512]{1,0:T(8,128)} %bitcast.276, pred[512,512]{1,0:T(8,128)(4,1)} %compare_or_fusion.1, bf16[512,12,64]{0,2,1:T(8,128)(2,1)} %bitcast.255, bf16[512,12,64]{2,1,0:T(8,128)(2,1)} %bitcast.263), kind=kOutput, calls=%fused_computation.29 | convolution fusion | flops 818282496 | bytes 5791744 | tf_op jit(solution)/shard_map/while/body/eval_jaxpr/cond/branch_1_fun/shqk,skhd->sqhd/dot_general | solution.py:159
  154.2 20.3 %while.68 = (s32[]{:T(128)}, f32[1,12,512]{2,1,0:T(8,128)}, s32[2]{0:T(128)}, s32[]{:T(128)}, s32[2,1,512]{2,1,0:T(1,128)S(1)}, /*index=5*/s32[]{:T(128)}, s32[1...) while((s32[]{:T(128)}, f32[1,12,512]{2,1,0:T(8,128)}, ...), condition=%wide.region_24.25_spmd.clone, body=%wide.region_19.24_spmd.clone.sunk | while | flops 822872576 | bytes 41666984 | solution.py:242
  164.1 10.5 %conditional.14 = (f32[1,12,512]{2,1,0:T(8,128)}) conditional(s32[]{:T(128)} %convert_element_type.282, f32[1,12,512]{2,1,0:T(8,128)} %get-tuple-element.2144, (s32[1,512]{1,0:T(1,128)S(1)}, s32[1,1,512]{2,1,0:T(1,128)S(1)}, s32[]{:T(128)}, s32[512]{0:T(512)S(1)}, s32[]{:T(128)}, /*index=5*/bf16[2,1,512,1536]{2,3,1,0:T(8,128)(2,1)}, s32[]{:T(128)}, ...), branch_computations={%region_21.21_spmd, %region_22.23_spmd} | conditional | flops 822872064 | bytes 41660532 | solution.py:240
  179.4 40.1 %while.69 = (s32[]{:T(128)}, f32[1,512,12,64]{1,3,2,0:T(8,128)}, f32[2,1,512,1536]{2,3,1,0:T(8,128)}, s32[2]{0:T(128)}, s32[]{:T(128)}, /*index=5*/s32[2,1,512]{...) while((s32[]{:T(128)}, f32[1,512,12,64]{1,3,2,0:T(8,128)}, ...), condition=%wide.region_29.30_spmd.clone, body=%wide.region_25.29_spmd.clone.sunk | while | flops 2050886144 | bytes 144902832 | solution.py:281
  189.5 30.1 %conditional.15 = ((f32[1,512,12,64]{1,3,2,0:T(8,128)}, f32[2,1,512,1536]{2,3,1,0:T(8,128)})) conditional(s32[]{:T(128)} %convert_element_type.283, (f32[1,512,12,64]{1,3,2,0:T(8,128)}, f32[2,1,512,1536]{2,3,1,0:T(8,128)}) %tuple.238, (bf16[2,1,512,1536]{2,3,1,0:T(8,128)(2,1)}, s32[]{:T(128)}, s32[1,512]{1,0:T(1,128)S(1)}, ...), branch_computations={%region_27.27_spmd, %region_28.28_spmd} | conditional | flops 2050885632 | bytes 144896320 | solution.py:278
  192.6 6.4 %fusion.54 = f32[12,512,512]{2,1,0:T(8,128)} fusion(bf16[512,12,64]{0,2,1:T(8,128)(2,1)S(1)} %bitcast.238, bf16[1,512,12,64]{1,3,2,0:T(8,128)(2,1)S(1)} %copy-done.3), kind=kOutput, calls=%fused_computation.74 | convolution fusion | flops 402653184 | bytes 14155776 | tf_op jit(solution)/shard_map/while/body/eval_jaxpr/cond/branch_1_fun/sqhd,skhd->shqk/dot_general | solution.py:41
  198.9 6.1 fusion.46
  205.1 7.3 %fusion.42 = bf16[12,512,512]{1,2,0:T(8,128)(2,1)S(1)} fusion(f32[12,512,512]{2,1,0:T(8,128)} %fusion.54, f32[12,512]{1,0:T(8,128)} %bitcast.39, f32[12,512]{1,0:T(8,128)S(1)} %bitcast.279, pred[512,512]{0,1:T(8,128)(4,1)S(1)} %compare_or_fusion.3, bf16[512,12,64]{0,2,1:T(8,128)(2,1)S(1)} %bitcast.254, bf16[1,512,12,64]{1,3,2,0:T(8,128)(2,1)} %get-tuple-element.1307), kind=kOutput, calls=%fused_computation.58 | convolution fusion | flops 424673280 | bytes 20758528 | tf_op jit(solution)/shard_map/while/body/eval_jaxpr/cond/branch_1_fun/sqhd,skhd->shqk/dot_general | solution.py:250
  219.5 6.6 %copy.51 = f32[2,1,512,1536]{3,2,1,0:T(8,128)} copy(f32[2,1,512,1536]{2,3,1,0:T(8,128)} %get-tuple-element.1350) | data formatting | bytes 12582912 | tf_op jit(solution)/shard_map/while | solution.py:281
  237.0 7.1 %convolution_convert_fusion.1 = bf16[768,3072]{1,0:T(8,128)(2,1)} fusion(bf16[512,3072]{1,0:T(8,128)(2,1)} %copy-done.75, f32[1,512,768]{2,1,0:T(8,128)S(1)} %copy-done.16, f32[768]{0:T(1024)S(1)} %copy-done.69, f32[768]{0:T(1024)S(1)} %copy-done.60, f32[512]{0:T(512)S(1)} %copy-done.65, f32[512]{0:T(512)S(1)} %copy-done.52), kind=kOutput, calls=%fused_computation.86 | convolution fusion | flops 2420244480 | bytes 9447424 | tf_op jit(solution)/shard_map/jtw,jth->wh/dot_general | solution.py:201
  244.1 7.8 %convolution_convert_fusion = bf16[3072,768]{1,0:T(8,128)(2,1)} fusion(f32[512,3072]{1,0:T(8,128)} %copy-done.74, bf16[1,512,768]{2,1,0:T(8,128)(2,1)S(1)} %copy-done.22, f32[512]{0:T(512)S(1)} %bitcast.288), kind=kOutput, calls=%fused_computation.85 | convolution fusion | flops 2424176640 | bytes 11798528 | tf_op jit(solution)/shard_map/ipr,iph->rh/dot_general | solution.py:191
  252.0 78.3 %collective-permute-done.4 = bf16[1,512,1536]{2,1,0:T(8,128)(2,1)} collective-permute-done((bf16[1,512,1536]{2,1,0:T(8,128)(2,1)}, bf16[1,512,1536]{2,1,0:T(8,128)(2,1)}, u32[]{:S(2)}, u32[]{:S(2)}) %collective-permute-start.4) | collective-permute-done | bytes 1572896 | tf_op jit(solution)/shard_map/ppermute | solution.py:19
  356.4 9.2 %fusion.79 = bf16[1,512,768]{2,1,0:T(8,128)(2,1)} fusion(f32[1,512,768]{2,1,0:T(8,128)} %copy-done.15, bf16[3072,768]{1,0:T(8,128)(2,1)} %param.34, f32[512,3072]{1,0:T(8,128)} %copy-done.74, f32[512]{0:T(512)} %bitcast.285), kind=kOutput, calls=%fused_computation.136 | convolution fusion | flops 2421817344 | bytes 13371392 | tf_op jit(solution)/shard_map/nxg,gi->nxi/dot_general | solution.py:185
  372.3 5.7 fusion.75
  389.8 44.6 %psum.36 = f32[9984]{0:T(1024)} all-reduce(f32[9984]{0:T(1024)} %constant_dynamic-update-slice_fusion), channel_id=1, replica_groups=mesh['seq'=8,'stream'=4] {'seq','stream'}, use_global_device_ids=true, to_apply=%region_40.41 | all-reduce | flops 9984 | bytes 79872 | tf_op jit(solution)/shard_map/psum | solution.py:323
  443.3 158.9 %all-reduce.9.cloned.1.call-done = (bf16[768,2304]{1,0:T(8,128)(2,1)}, bf16[768,768]{1,0:T(8,128)(2,1)}, bf16[768,3072]{1,0:T(8,128)(2,1)}, bf16[3072,768]{1,0:T(8,128)(2,1)}) async-done(((bf16[768,2304]{1,0:T(8,128)(2,1)}, bf16[768,768]{1,0:T(8,128)(2,1)}, bf16[768,3072]{1,0:T(8,128)(2,1)}, bf16[3072,768]{1,0:T(8,128)(2,1)}), (bf16[768,2304]{1,0:T(8,128)(2,1)}, bf16[768,768]{1,0:T(8,128)(2,1)}, ...) | async-done | bytes 14155792 | tf_op jit(solution)/shard_map/psum | solution.py:325
  609.8 5.0 convert_element_type.183
  (330 shorter events, 195.9 us)
Async XLA Ops:
  7.2 10.2 %copy-start = (bf16[768,2304]{1,0:T(8,128)(2,1)S(1)}, bf16[768,2304]{1,0:T(8,128)(2,1)}, u32[]{:S(2)}) copy-start(bf16[768,2304]{1,0:T(8,128)(2,1)} %param.30) | copy-start | bytes 10616836
  7.2 595.0 %all-reduce.9.cloned.1.call-start = ((), (), s32[]{:S(2)}) async-start(), calls=%async_computation | async-start | bytes 28311552 | tf_op jit(solution)/shard_map/psum | solution.py:325
  8.1 16.2 %collective-permute-start.2 = (s32[1,2]{1,0:T(1,128)S(1)}, s32[1,2]{1,0:T(1,128)S(1)}, u32[]{:S(2)}, u32[]{:S(2)}) collective-permute-start(s32[1,2]{1,0:T(1,128)S(1)} %slice.148), channel_id=1, source_target_pairs={{0,4},{4,8},{8,12},{12,16},{16,20},{20,24},{24,28},{1,5},{5,9},{9,... | collective-permute-start | bytes 32 | tf_op jit(solution)/shard_map/ppermute | solution.py:19
  20.7 4.9 collective-permute-start.1
  28.1 12.7 %copy-start.70 = (bf16[768]{0:T(1024)(128)(2,1)S(1)}, bf16[768]{0:T(1024)(128)(2,1)}, u32[]{:S(2)}) copy-start(bf16[768]{0:T(1024)(128)(2,1)} %param.37) | copy-start | bytes 4612
  28.1 13.3 %copy-start.71 = (bf16[768]{0:T(1024)(128)(2,1)S(1)}, bf16[768]{0:T(1024)(128)(2,1)}, u32[]{:S(2)}) copy-start(bf16[768]{0:T(1024)(128)(2,1)} %param.38) | copy-start | bytes 4612
  30.6 44.9 %collective-permute-start.3 = (bf16[1,512,1536]{2,1,0:T(8,128)(2,1)}, bf16[1,512,1536]{2,1,0:T(8,128)(2,1)}, u32[]{:S(2)}, u32[]{:S(2)}) collective-permute-start(bf16[1,512,1536]{2,1,0:T(8,128)(2,1)} %get-tuple-element.1713), channel_id=1, source_target_pairs={{0,4},{4,8},{8,12},{12,16},{16,20},{20,24},{24,28},{1,5},{5,9},{9,... | collective-permute-start | bytes 4718600 | tf_op jit(solution)/shard_map/ppermute | solution.py:19
  35.9 31.4 %collective-permute-start = (s32[1,512]{1,0:T(1,128)S(1)}, s32[1,512]{1,0:T(1,128)S(1)}, u32[]{:S(2)}, u32[]{:S(2)}) collective-permute-start(s32[1,512]{1,0:T(1,128)S(1)} %copy-done.24), channel_id=1, source_target_pairs={{0,4},{4,8},{8,12},{12,16},{16,20},{20,24},{24,28},{1,5},{5,9},{9,... | collective-permute-start | bytes 6152 | tf_op jit(solution)/shard_map/ppermute | solution.py:19
  136.4 10.1 %copy-start.15 = (f32[1,512,768]{2,1,0:T(8,128)}, f32[1,512,768]{2,1,0:T(8,128)S(1)}, u32[]{:S(2)}) copy-start(f32[1,512,768]{2,1,0:T(8,128)S(1)} %get-tuple-element.1723) | copy-start | bytes 4718596
  136.4 10.1 %copy-start.51 = (f32[512]{0:T(512)}, f32[512]{0:T(512)S(1)}, u32[]{:S(2)}) copy-start(f32[512]{0:T(512)S(1)} %broadcast_multiply_fusion.1) | copy-start | bytes 6148
  136.9 9.7 %copy-start.64 = (f32[512]{0:T(512)}, f32[512]{0:T(512)S(1)}, u32[]{:S(2)}) copy-start(f32[512]{0:T(512)S(1)} %fusion.91) | copy-start | bytes 6148
  229.3 101.1 %collective-permute-start.4 = (bf16[1,512,1536]{2,1,0:T(8,128)(2,1)}, bf16[1,512,1536]{2,1,0:T(8,128)(2,1)}, u32[]{:S(2)}, u32[]{:S(2)}) collective-permute-start(bf16[1,512,1536]{2,1,0:T(8,128)(2,1)} %fusion.76), channel_id=1, source_target_pairs={{4,0},{8,4},{12,8},{16,12},{20,16},{24,20},{28,24},{5,1},{9,5},{13... | collective-permute-start | bytes 4718600 | tf_op jit(solution)/shard_map/ppermute | solution.py:19
  237.0 93.3 %slice-start.4 = ((s8[6291456]{0:T(1024)(128)(4,1)}), s8[4194304]{0:T(1024)(128)(4,1)S(1)}, s32[]{:S(2)}) async-start(s8[6291456]{0:T(1024)(128)(4,1)} %bitcast.258), calls=%async_computation.5 | async-start | bytes 8388608
  237.0 95.2 %slice-start = ((s8[4718592]{0:T(1024)(128)(4,1)}), s8[4194304]{0:T(1024)(128)(4,1)S(1)}, s32[]{:S(2)}) async-start(s8[4718592]{0:T(1024)(128)(4,1)} %bitcast.247), calls=%async_computation.1 | async-start | bytes 8388608
  244.1 86.2 %slice-start.5 = ((s8[6291456]{0:T(1024)(128)(4,1)}), s8[2097152]{0:T(1024)(128)(4,1)S(1)}, s32[]{:S(2)}) async-start(s8[6291456]{0:T(1024)(128)(4,1)} %bitcast.258), calls=%async_computation.6 | async-start | bytes 4194304
  244.1 88.1 %slice-start.1 = ((s8[4718592]{0:T(1024)(128)(4,1)}), s8[524288]{0:T(1024)(128)(4,1)S(1)}, s32[]{:S(2)}) async-start(s8[4718592]{0:T(1024)(128)(4,1)} %bitcast.247), calls=%async_computation.2 | async-start | bytes 1048576
  252.0 80.3 %copy-start.30 = (f32[2304]{0:T(1024)S(1)}, f32[2304]{0:T(1024)}, u32[]{:S(2)}) copy-start(f32[2304]{0:T(1024)} %copy-done.29) | copy-start | bytes 27652
  252.0 80.3 %copy-start.32 = (f32[2304]{0:T(1024)S(1)}, f32[2304]{0:T(1024)}, u32[]{:S(2)}) copy-start(f32[2304]{0:T(1024)} %copy-done.31) | copy-start | bytes 27652
  252.0 80.3 %copy-start.34 = (f32[2304]{0:T(1024)S(1)}, f32[2304]{0:T(1024)}, u32[]{:S(2)}) copy-start(f32[2304]{0:T(1024)} %copy-done.33) | copy-start | bytes 27652
  252.0 80.3 %copy-start.36 = (f32[1,2,2304]{2,1,0:T(2,128)S(1)}, f32[1,2,2304]{2,1,0:T(2,128)}, u32[]{:S(2)}) copy-start(f32[1,2,2304]{2,1,0:T(2,128)} %copy-done.35) | copy-start | bytes 55300
  252.0 80.3 %copy-start.56 = (f32[1,512]{1,0:T(1,128)S(1)}, f32[1,512]{1,0:T(1,128)}, u32[]{:S(2)}) copy-start(f32[1,512]{1,0:T(1,128)} %copy-done.55) | copy-start | bytes 6148
  252.0 80.3 %copy-start.58 = (f32[1,512]{1,0:T(1,128)S(1)}, f32[1,512]{1,0:T(1,128)}, u32[]{:S(2)}) copy-start(f32[1,512]{1,0:T(1,128)} %copy-done.57) | copy-start | bytes 6148
  339.6 6.9 %collective-permute-start.5 = (f32[1,2,2304]{2,1,0:T(2,128)S(1)}, f32[1,2,2304]{2,1,0:T(2,128)S(1)}, u32[]{:S(2)}, u32[]{:S(2)}) collective-permute-start(f32[1,2,2304]{2,1,0:T(2,128)S(1)} %pad_add_fusion.2), channel_id=1, source_target_pairs={{4,0},{8,4},{12,8},{16,12},{20,16},{24,20},{28,24},{5,1},{9,5},{13... | collective-permute-start | bytes 55304 | tf_op jit(solution)/shard_map/ppermute | solution.py:19
  378.0 61.1 %copy-start.49 = (f32[512]{0:T(512)S(1)}, f32[512]{0:T(512)}, u32[]{:S(2)}) copy-start(f32[512]{0:T(512)} %copy-done.48) | copy-start | bytes 6148
  (69 other events, 278.2 us)
Sparse Core Ops, SparseCore 0:
  351.4 250.7 all-reduce.8

commit v2 on v0

v2 whole, which is shorter than its diff:
```python
import jax
import jax.numpy as jnp
from jax import lax
from jax.experimental import pallas as pl
from jax.experimental.pallas import tpu as pltpu
from jax.sharding import PartitionSpec as P

HD = 64
PAIR = 2 * HD
EPSILON = 1e-05
MASKED = -1e30
REACH = 256
TILE = 128
WINDOW = REACH + TILE


def layer_norm(field, gain, shift):
    center = field - jnp.mean(field, -1, keepdims=True)
    spread = jnp.mean(center * center, -1, keepdims=True)
    return center * lax.rsqrt(spread + EPSILON) * gain + shift


def dot(left, right, left_dim, right_dim):
    return lax.dot_general(
        left, right, (((left_dim,), (right_dim,)), ((), ())), preferred_element_type=jnp.float32
    )


def both_heads(rows):
    first = lax.broadcasted_iota(jnp.int32, rows.shape, 1) < HD
    zero = jnp.zeros_like(rows)
    return jnp.concatenate([jnp.where(first, rows, zero), jnp.where(first, zero, rows)], 0)


def own_lanes(rows):
    half = rows.shape[0] // 2
    first = lax.broadcasted_iota(jnp.int32, (half, rows.shape[1]), 1) < HD
    return jnp.where(first, rows[:half], rows[half:])


def attend_kernel(
    uq, uk, uv, kq, kk, kv, same_one, same_two, key_ids, query_ids, out, probs, cq, ck, cv, bias
):
    tiles = query_ids.shape[1] // TILE

    @pl.when(pl.program_id(0) == 0)
    def _():
        for t in range(tiles):
            rows = lax.broadcasted_iota(jnp.int32, (WINDOW, TILE), 0)
            columns = lax.broadcasted_iota(jnp.int32, (WINDOW, TILE), 1) + REACH
            equal = key_ids[t * TILE : t * TILE + WINDOW] == query_ids[:, t * TILE : (t + 1) * TILE]
            allowed = (equal & (rows <= columns)) | (rows == columns)
            tile_bias = jnp.where(allowed, 0.0, MASKED)
            bias[t] = jnp.concatenate([tile_bias, tile_bias], 1)

    one, two = same_one[...], same_two[...]

    def convolved(u, taps):
        field = u[...].astype(jnp.float32)
        return (
            taps[0:1] * field
            + taps[1:2] * pltpu.roll(field, 1, 0) * one
            + taps[2:3] * pltpu.roll(field, 2, 0) * two
        )

    cq[...] = convolved(uq, kq)[REACH:].astype(jnp.bfloat16) * 0.125
    ck[...] = convolved(uk, kk).astype(jnp.bfloat16)
    cv[...] = convolved(uv, kv).astype(jnp.bfloat16)
    for t in range(tiles):
        window = slice(t * TILE, t * TILE + WINDOW)
        own = slice(t * TILE, (t + 1) * TILE)
        scores = dot(ck[window], both_heads(cq[own]), 1, 1) + bias[t]
        powers = jnp.exp(scores - jnp.max(scores, 0, keepdims=True))
        narrow = (powers * (1.0 / jnp.sum(powers, 0, keepdims=True))).astype(jnp.bfloat16)
        probs[0, t] = narrow
        out[own] = own_lanes(dot(narrow, cv[window], 0, 0)).astype(jnp.bfloat16)


def attend_back_kernel(
    grad_out, probs, cq, ck, cv, uq, uk, uv, kq, kk, kv, same_one, same_two,
    gu, gtaps, gq_rows, gk_rows, gv_rows,
):
    head = pl.program_id(0)
    width = gu.shape[1] // 3
    tiles = grad_out.shape[0] // TILE
    gq_rows[:REACH] = jnp.zeros((REACH, PAIR), jnp.float32)
    gk_rows[...] = jnp.zeros_like(gk_rows)
    gv_rows[...] = jnp.zeros_like(gv_rows)
    for t in range(tiles):
        window = slice(t * TILE, t * TILE + WINDOW)
        own = slice(t * TILE, (t + 1) * TILE)
        grads = both_heads(grad_out[own])
        narrow = probs[0, t]
        wide = narrow.astype(jnp.float32)
        grad_probs = dot(cv[window], grads, 1, 1)
        delta = jnp.sum(wide * grad_probs, 0, keepdims=True)
        grad_scores = (wide * (grad_probs - delta)).astype(jnp.bfloat16)
        gk_rows[window] += dot(grad_scores, both_heads(cq[own]), 1, 0)
        gv_rows[window] += dot(narrow, grads, 1, 0)
        gq_rows[REACH + t * TILE : REACH + (t + 1) * TILE] = (
            own_lanes(dot(grad_scores, ck[window], 0, 0)) * 0.125
        )
    one, two = same_one[...], same_two[...]
    last = gq_rows.shape[0]
    for part, (rows, u, taps) in enumerate(
        ((gq_rows, uq, kq), (gk_rows, uk, kk), (gv_rows, uv, kv))
    ):
        field = u[...].astype(jnp.float32)
        grad = rows[...]
        grad_one, grad_two = grad * one, grad * two
        place = pl.ds(pl.multiple_of(part * width + head * PAIR, PAIR), PAIR)
        gu[:, place] = (
            taps[0:1] * grad
            + taps[1:2] * pltpu.roll(grad_one, last - 1, 0)
            + taps[2:3] * pltpu.roll(grad_two, last - 2, 0)
        ).astype(jnp.bfloat16)
        gtaps[0:1, place] = jnp.sum(grad * field, 0, keepdims=True)
        gtaps[1:2, place] = jnp.sum(grad_one * pltpu.roll(field, 1, 0), 0, keepdims=True)
        gtaps[2:3, place] = jnp.sum(grad_two * pltpu.roll(field, 2, 0), 0, keepdims=True)


def column_specs(rows, pairs):
    return [
        pl.BlockSpec((rows, PAIR), lambda h, part=part: (0, part * pairs + h)) for part in range(3)
    ]


def whole(shape):
    return pl.BlockSpec(shape, lambda h: (0,) * len(shape))


def attend(mixed, taps, same_one, same_two, key_ids, query_ids):
    rows, width = mixed.shape[0], mixed.shape[1] // 3
    slots, pairs = rows - REACH, width // PAIR
    tiles = slots // TILE
    block = lambda count: pl.BlockSpec((count, PAIR), lambda h: (0, h))
    return pl.pallas_call(
        attend_kernel,
        grid=(pairs,),
        in_specs=column_specs(rows, pairs)
        + column_specs(3, pairs)
        + [whole((rows, 1))] * 3
        + [whole((1, slots))],
        out_specs=[
            block(slots),
            pl.BlockSpec((1, tiles, WINDOW, 2 * TILE), lambda h: (h, 0, 0, 0)),
            block(slots),
            block(rows),
            block(rows),
        ],
        out_shape=[
            jax.ShapeDtypeStruct((slots, width), jnp.bfloat16),
            jax.ShapeDtypeStruct((pairs, tiles, WINDOW, 2 * TILE), jnp.bfloat16),
            jax.ShapeDtypeStruct((slots, width), jnp.bfloat16),
            jax.ShapeDtypeStruct((rows, width), jnp.bfloat16),
            jax.ShapeDtypeStruct((rows, width), jnp.bfloat16),
        ],
        scratch_shapes=[pltpu.VMEM((tiles, WINDOW, 2 * TILE), jnp.float32)],
        name="attend",
    )(mixed, mixed, mixed, taps, taps, taps, same_one, same_two, key_ids, query_ids)


def attend_back(grad_heads, kept, mixed, taps, same_one, same_two):
    rows, width = mixed.shape[0], mixed.shape[1] // 3
    slots, pairs = rows - REACH, width // PAIR
    tiles = slots // TILE
    probs, cq, ck, cv = kept
    block = lambda count: pl.BlockSpec((count, PAIR), lambda h: (0, h))
    return pl.pallas_call(
        attend_back_kernel,
        grid=(pairs,),
        in_specs=[
            block(slots),
            pl.BlockSpec((1, tiles, WINDOW, 2 * TILE), lambda h: (h, 0, 0, 0)),
            block(slots),
            block(rows),
            block(rows),
        ]
        + column_specs(rows, pairs)
        + column_specs(3, pairs)
        + [whole((rows, 1))] * 2,
        out_specs=[whole((rows, 3 * width)), whole((3, 3 * width))],
        out_shape=[
            jax.ShapeDtypeStruct((rows, 3 * width), jnp.bfloat16),
            jax.ShapeDtypeStruct((3, 3 * width), jnp.float32),
        ],
        scratch_shapes=[pltpu.VMEM((rows, PAIR), jnp.float32)] * 3,
        name="attend_back",
    )(grad_heads, probs, cq, ck, cv, mixed, mixed, mixed, taps, taps, taps, same_one, same_two)


def passed_along(block, axis, distance):
    devices = range(lax.axis_size(axis))
    route = [(i - distance, i) for i in devices if i - distance in devices]
    return lax.ppermute(block, axis, route)


def summed(grads, small):
    both = ("seq", "stream")
    small_sum = lax.psum(jnp.concatenate([piece.reshape(-1) for piece in small]), both)
    big = [lax.psum(piece, both).astype(jnp.float32) for piece in grads]
    parts, offset = [], 0
    for piece in small:
        parts.append(small_sum[offset : offset + piece.size].reshape(piece.shape))
        offset += piece.size
    return big, parts


def product(left, right, left_dim, right_dim, dtype=jnp.float32):
    return dot(left, right, left_dim, right_dim).astype(dtype)


def on_device(
    tokens,
    segment_ids,
    query_key_value_weight,
    conv_kernel,
    attention_output_weight,
    up_weight,
    down_weight,
    gain_attn,
    shift_attn,
    gain_ffn,
    shift_ffn,
    cotangent,
):
    narrow = jnp.bfloat16
    own_tokens, ids, grad_low = tokens[0], segment_ids[0], cotangent[0]
    prior_tokens, prior_ids = passed_along((own_tokens[-REACH:], ids[-REACH:]), "seq", 1)
    prior_ids = jnp.where(lax.axis_index("seq") > 0, prior_ids, -1)
    rows_ids = jnp.concatenate([prior_ids, ids])
    live_rows = rows_ids >= 0

    def same(distance):
        moved = jnp.concatenate([jnp.full((distance,), -1, jnp.int32), rows_ids[:-distance]])
        return ((moved == rows_ids) & live_rows).astype(jnp.float32)[:, None]

    same_one, same_two = same(1), same(2)
    key_ids = jnp.where(live_rows, rows_ids, -2)[:, None]
    live = (ids >= 0).astype(jnp.float32)[:, None]
    taps = conv_kernel.astype(jnp.float32)

    rows = jnp.concatenate([prior_tokens, own_tokens]).astype(jnp.float32)
    first, first_back = jax.vjp(
        layer_norm, rows, gain_attn.astype(jnp.float32), shift_attn.astype(jnp.float32)
    )
    first = first.astype(narrow)
    mixed = product(first, query_key_value_weight, 1, 0, narrow)
    attended, *kept = attend(mixed, taps, same_one, same_two, key_ids, ids[None])

    middle = own_tokens.astype(jnp.float32) + live * product(attended, attention_output_weight, 1, 0)
    second, second_back = jax.vjp(
        layer_norm, middle, gain_ffn.astype(jnp.float32), shift_ffn.astype(jnp.float32)
    )
    second = second.astype(narrow)
    hidden = jnp.maximum(product(second, up_weight, 1, 0), 0.0)
    active = jnp.square(hidden).astype(narrow)
    grad = grad_low.astype(jnp.float32)
    grad_branch = (live * grad).astype(narrow)
    grad_w_down = product(active, grad_branch, 0, 0, narrow)
    grad_hidden = (product(grad_branch, down_weight, 1, 1) * (2.0 * hidden)).astype(narrow)
    grad_w_up = product(second, grad_hidden, 0, 0, narrow)
    out_tokens = (middle + live * product(active, down_weight, 1, 0)).astype(narrow)
    grad_part, grad_gain_ffn, grad_shift_ffn = second_back(product(grad_hidden, up_weight, 1, 1))
    grad_middle = grad + grad_part
    grad_attended = (live * grad_middle).astype(narrow)
    grad_w_out = product(attended, grad_attended, 0, 0, narrow)
    grad_heads = product(grad_attended, attention_output_weight, 1, 1, narrow)

    grad_mixed, grad_taps = attend_back(grad_heads, kept, mixed, taps, same_one, same_two)
    grad_w_qkv = product(first, grad_mixed, 0, 0, narrow)
    grad_rows, grad_gain_attn, grad_shift_attn = first_back(
        product(grad_mixed, query_key_value_weight, 1, 1)
    )
    later = passed_along(grad_rows[:REACH].astype(narrow), "seq", -1)
    grad_tokens = grad_middle + grad_rows[REACH:]
    slots = grad_tokens.shape[0]
    grad_tokens = grad_tokens + jnp.pad(
        later.astype(jnp.float32), ((slots - REACH, 0), (0, 0))
    )
    big, parts = summed(
        [grad_w_down, grad_w_up, grad_w_out, grad_w_qkv],
        [grad_taps, grad_gain_attn, grad_shift_attn, grad_gain_ffn, grad_shift_ffn],
    )
    return (
        out_tokens[None],
        grad_tokens[None],
        big[3],
        parts[0],
        big[2],
        big[1],
        big[0],
        parts[1],
        parts[2],
        parts[3],
        parts[4],
    )


def solution(mesh):
    return jax.shard_map(
        on_device,
        mesh=mesh,
        in_specs=(
            P("stream", "seq", None),
            P("stream", "seq"),
            P(),
            P(),
            P(),
            P(),
            P(),
            P(),
            P(),
            P(),
            P(),
            P("stream", "seq", None),
        ),
        out_specs=(
            P("stream", "seq", None),
            P("stream", "seq", None),
            P(),
            P(),
            P(),
            P(),
            P(),
            P(),
            P(),
            P(),
            P(),
        ),
        check_vma=False,
    )
```

time: 1620 us -> 392 us (0.24); the launches traced: 1590 us -> 390 us
  waiting for transfers between devices: 1010 us -> 175 us
  local copies, waits for them, and re-layouts: 363 us -> 20.3 us
  blocking collectives: 0 us -> 42.7 us
  matrix products: 86.2 us -> 53.9 us
  loops' own time: 30.1 us -> 0 us
  Pallas kernels: 0 us -> 29.1 us
  other arithmetic: 62.4 us -> 43.8 us
    unnamed x5 -> x1, waiting for transfers between devices: 877 us -> 0.02 us
    unnamed x174 -> x59, local copies, waits for them, and re-layouts: 228 us -> 7.99 us
    psum x1, waiting for transfers between devices: 44.8 us -> 175 us  [summed(): big = [lax.psum(piece, both).astype(jnp.float32) for piece in grads]]
    ppermute x6 -> x3, waiting for transfers between devices: 87.7 us -> 0.01 us  [passed_along(): return lax.ppermute(block, axis, route)]
    psum x0 -> x1, blocking collectives: none -> 42.7 us  [summed(): lax.psum(jnp.concatenate([piece.reshape(-1) for piece in small]), both)]
    reshape x7 -> x2, local copies, waits for them, and re-layouts: 41.7 us -> 2.77 us  [the longest x1 1.39 us: summed(): piece.reshape(-1)]
    slice x17 -> x5, local copies, waits for them, and re-layouts: 43.8 us -> 6.14 us  [the longest x2 2.74 us: summed(): parts.append(small_sum[offset:offset + piece.size].reshape(piece.shape))]
    dot_general x21 -> x12, matrix products: 86.2 us -> 53.9 us  [dot(): lax.dot_general(left, right, (((left_dim,), (right_dim,)), ((), ())), pre...]
  transfers between devices with their start and end apart: 9 -> 4, of which waited for: 6 -> 1; matrix products, arithmetic and copies ran while one was open for 4% -> 13% of each run, Pallas kernels for 0% -> 0%
where the time goes in v2:
time: 392 us; the launch traced here: 390 us
  waiting for transfers between devices  175 us (45%)
  matrix products  53.9 us (14%)
  other arithmetic  43.8 us (11%)
  blocking collectives  42.7 us (11%)
  Pallas kernels  29.1 us (7%)
  local copies, waits for them, and re-layouts  20.3 us (5%)
  between operations  14.4 us (4%)
  starting transfers between devices  10.8 us (3%)
    psum x1, waiting for transfers between devices, summed(): big = [lax.psum(piece, both).astype(jnp.float32) for piece in grads]  175 us
    dot_general x12, matrix products, dot(): lax.dot_general(left, right, (((left_dim,), (right_dim,)), ((), ())), pre...  53.9 us
    psum x1, blocking collectives, summed(): lax.psum(jnp.concatenate([piece.reshape(-1) for piece in small]), both)  42.7 us
    pallas_call x1, Pallas kernels, attend_back(): pl.pallas_call(attend_back_kernel, grid=(pairs,), in_specs=[block(slots),...  16.6 us
    convert_element_type x4, other arithmetic, summed(): big = [lax.psum(piece, both).astype(jnp.float32) for piece in grads]  16.6 us
    pallas_call x1, Pallas kernels, attend(): pl.pallas_call(attend_kernel, grid=(pairs,), in_specs=column_specs(rows,...  12.4 us
    ppermute x3, starting transfers between devices, passed_along(): return lax.ppermute(block, axis, route)  10.7 us
    unnamed x59, local copies, waits for them, and re-layouts  7.99 us
  transfers between devices with their start and end apart: 4, of which 1 were waited for; matrix products, arithmetic and copies ran while one was open for 13% of the time, Pallas kernels for 0%

profile of v2, /device:TPU:0, one launch (start us, length us, event | category | flops | bytes accessed | tf_op | source)
XLA Modules:
  0.0 390.3 jit_solution(17216831894113515097)
XLA Ops:
  8.1 5.0 %collective-permute-start.1 = (s32[256]{0:T(256)S(1)}, s32[256]{0:T(256)S(1)}, u32[]{:S(2)}, u32[]{:S(2)}) collective-permute-start(s32[256]{0:T(256)S(1)} %bitcast.53), channel_id=1, source_target_pairs={{0,4},{4,8},{8,12},{12,16},{16,20},{20,24},{24,28},{1,5},{5,9},{9,... | collective-permute-start | bytes 3080 | tf_op jit(solution)/shard_map/ppermute | solution.py:195
  14.8 4.2 %collective-permute-start = (bf16[256,768]{1,0:T(8,128)(2,1)}, bf16[256,768]{1,0:T(8,128)(2,1)}, u32[]{:S(2)}, u32[]{:S(2)}) collective-permute-start(bf16[256,768]{1,0:T(8,128)(2,1)} %slice_bitcast_fusion), channel_id=1, source_target_pairs={{0,4},{4,8},{8,12},{12,16},{16,20},{20,24},{24,28},{1,5},{5,9},{9,... | collective-permute-start | bytes 1179656 | tf_op jit(solution)/shard_map/ppermute | solution.py:195
  33.1 1.9 fusion.15.same_one
  37.7 6.1 %convolution_convert_fusion.1.uq.uk.uv = bf16[768,2304]{1,0:T(8,128)(2,1)} fusion(bf16[768,2304]{1,0:T(8,128)(2,1)S(1)} %copy-done, f32[768]{0:T(1024)S(1)} %copy-done.15, f32[768]{0:T(1024)S(1)} %convert_element_type.103, f32[768]{0:T(1024)S(1)} %fusion.20, f32[768]{0:T(1024)S(1)} %broadcast_multiply_fusion, bf16[512,768]{1,0:T(8,128)(2,1)S(1)} %bitcast.41, ...), kind=kOutput, calls=%fused_computation.3 | convolution fusion | flops 2724986880 | bytes 8269824 | tf_op jit(solution)/shard_map/dot_general | solution.py:24
  43.8 12.4 %attend.1 = (bf16[512,768]{1,0:T(8,128)(2,1)}, bf16[6,4,384,256]{3,2,1,0:T(8,128)(2,1)}, bf16[512,768]{1,0:T(8,128)(2,1)}, bf16[768,768]{1,0:T(8,128)(2,1)}, bf16[768,768]{1,0:T(8,128)(2,1)}) custom-call(bf16[768,2304]{1,0:T(8,128)(2,1)} %convolution_convert_fusion.1.uq.uk.uv, bf16[768,2304]{1,0:T(8,128)(2,1)} %convolution_convert_fusion.1.uq.uk.uv, ...), custom_call_target="tpu_custom_call" | custom-call | tf_op jit(solution)/shard_map/attend/pallas_call | solution.py:137
  56.3 2.6 fusion.31
  59.3 4.9 %fusion.26 = f32[512,3072]{1,0:T(8,128)S(1)} fusion(bf16[768,3072]{1,0:T(8,128)(2,1)} %param.17, f32[512,768]{1,0:T(8,128)S(1)} %get-tuple-element.43, f32[768]{0:T(1024)S(1)} %copy-done.16, f32[768]{0:T(1024)S(1)} %copy-done.12, f32[512]{0:T(512)S(1)} %fusion.21, f32[512]{0:T(512)S(1)} %broadcast_multiply_fusion.1), kind=kOutput, calls=%fused_computation.69 | convolution fusion | flops 2417885184 | bytes 12593152 | tf_op jit(solution)/shard_map/dot_general | solution.py:24
  64.3 4.5 %convolution_convert_fusion.2 = bf16[3072,768]{1,0:T(8,128)(2,1)} fusion(f32[512,3072]{1,0:T(8,128)S(1)} %fusion.26, bf16[1,512,768]{2,1,0:T(8,128)(2,1)S(1)} %copy-done.9, f32[512]{0:T(512)S(1)} %copy-done.13), kind=kOutput, calls=%fused_computation.4 | convolution fusion | flops 2424176640 | bytes 11798528 | tf_op jit(solution)/shard_map/dot_general | solution.py:24
  69.5 3.0 multiply_convert_fusion
  72.6 3.5 multiply_reduce_fusion
  76.1 4.7 %convolution_convert_fusion.3 = bf16[768,3072]{1,0:T(8,128)(2,1)} fusion(bf16[512,3072]{1,0:T(8,128)(2,1)S(1)} %multiply_convert_fusion, f32[512,768]{1,0:T(8,128)S(1)} %get-tuple-element.43, f32[768]{0:T(1024)S(1)} %copy-done.16, f32[768]{0:T(1024)S(1)} %copy-done.12, f32[512]{0:T(512)S(1)} %fusion.21, f32[512]{0:T(512)S(1)} %broadcast_multiply_fusion.1), kind=kOutput, calls=%fused_computation.5 | convolution fusion | flops 2420244480 | bytes 9447424 | tf_op jit(solution)/shard_map/dot_general | solution.py:24
  86.7 16.6 %attend_back.1 = (bf16[768,2304]{1,0:T(8,128)(2,1)}, f32[3,2304]{1,0:T(4,128)}) custom-call(bf16[512,768]{1,0:T(8,128)(2,1)} %convolution_convert_fusion.5.grad_out, bf16[6,4,384,256]{3,2,1,0:T(8,128)(2,1)} %get-tuple-element.19.probs, bf16[512,768]{1,0:T(8,128)(2,1)} %get-tuple-element.20.cq, bf16[768,768]{1,0:T(8,128)(2,1)} %get-tuple-element.21.ck, ...), custom_call_target="tpu_custom_call" | custom-call | tf_op jit(solution)/shard_map/attend_back/pallas_call | solution.py:169
  103.4 7.4 %convolution_convert_fusion = bf16[768,2304]{1,0:T(8,128)(2,1)} fusion(bf16[768,2304]{1,0:T(8,128)(2,1)} %get-tuple-element.23, f32[768]{0:T(1024)} %convert_element_type.104, f32[768]{0:T(1024)S(1)} %convert_element_type.103, f32[768]{0:T(1024)S(1)} %fusion.20, f32[768]{0:T(1024)S(1)} %broadcast_multiply_fusion, bf16[512,768]{1,0:T(8,128)(2,1)} %bitcast.37, ...), kind=kOutput, calls=%fused_computation.2 | convolution fusion | flops 2724986880 | bytes 8269824 | tf_op jit(solution)/shard_map/dot_general | solution.py:24
  113.5 5.5 %fusion.28 = (f32[768]{0:T(1024)S(1)}, f32[768]{0:T(1024)S(1)}, f32[768,768]{1,0:T(8,128)S(1)}) fusion(f32[768]{0:T(1024)S(1)} %convert_element_type.103, f32[768]{0:T(1024)S(1)} %broadcast_multiply_fusion, bf16[512,768]{1,0:T(8,128)(2,1)} %bitcast.38, bf16[256,768]{1,0:T(8,128)(2,1)} %collective-permute-done, bf16[768,2304]{1,0:T(8,128)(2,1)} %get-tuple-element.23, ...), kind=kOutput, calls=%fused_computation.71 | convolution fusion | flops 2723215872 | bytes 10629120 | tf_op jit(solution)/shard_map/dot_general | solution.py:24
  119.1 2.7 fusion.8
  123.1 2.3 broadcast_add_fusion
  130.4 8.0 %fusion.14 = bf16[1,512,768]{2,1,0:T(8,128)(2,1)} fusion(f32[512,768]{1,0:T(8,128)S(1)} %copy-done.6, bf16[3072,768]{1,0:T(8,128)(2,1)} %param.18, f32[512,3072]{1,0:T(8,128)} %copy-done.21, f32[512]{0:T(512)S(1)} %copy-done.14), kind=kOutput, calls=%fused_computation.36 | convolution fusion | flops 2421817344 | bytes 13371392 | tf_op jit(solution)/shard_map/dot_general | solution.py:24
  140.3 42.7 %psum.36 = f32[9984]{0:T(1024)} all-reduce(f32[9984]{0:T(1024)} %constant_dynamic-update-slice_fusion), channel_id=1, replica_groups=mesh['seq'=8,'stream'=4] {'seq','stream'}, use_global_device_ids=true, to_apply=%region_13.14 | all-reduce | flops 9984 | bytes 79872 | tf_op jit(solution)/shard_map/psum | solution.py:200
  187.1 3.8 fusion.13
  190.9 175.4 %all-reduce.5.cloned.1.call-done = (bf16[768,2304]{1,0:T(8,128)(2,1)}, bf16[768,768]{1,0:T(8,128)(2,1)}, bf16[768,3072]{1,0:T(8,128)(2,1)}, bf16[3072,768]{1,0:T(8,128)(2,1)}) async-done(((bf16[768,2304]{1,0:T(8,128)(2,1)}, bf16[768,768]{1,0:T(8,128)(2,1)}, bf16[768,3072]{1,0:T(8,128)(2,1)}, bf16[3072,768]{1,0:T(8,128)(2,1)}), (bf16[768,2304]{1,0:T(8,128)(2,1)}, bf16[768,768]{1,0:T(8,128)(2,1)}, ...) | async-done | bytes 14155792 | tf_op jit(solution)/shard_map/psum | solution.py:201
  366.3 3.0 convert_element_type.123
  369.3 4.1 %convert_element_type.121 = f32[768,2304]{1,0:T(8,128)} convert(bf16[768,2304]{1,0:T(8,128)(2,1)S(1)} %copy-done.8) | non-fusion elementwise | flops 1769472 | bytes 10616832 | tf_op jit(solution)/shard_map/convert_element_type | solution.py:201
  373.9 5.0 %convert_element_type.125 = f32[768,3072]{1,0:T(8,128)} convert(bf16[768,3072]{1,0:T(8,128)(2,1)S(1)} %copy-done.7) | non-fusion elementwise | flops 2359296 | bytes 14155776 | tf_op jit(solution)/shard_map/convert_element_type | solution.py:201
  378.9 4.5 %convert_element_type.127 = f32[3072,768]{1,0:T(8,128)} convert(bf16[3072,768]{1,0:T(8,128)(2,1)S(1)} %bitcast.45) | non-fusion elementwise | flops 2359296 | bytes 14155776 | tf_op jit(solution)/shard_map/convert_element_type | solution.py:201
  (108 shorter events, 41.9 us)
Async XLA Ops:
  7.2 30.5 %copy-start = (bf16[768,2304]{1,0:T(8,128)(2,1)S(1)}, bf16[768,2304]{1,0:T(8,128)(2,1)}, u32[]{:S(2)}) copy-start(bf16[768,2304]{1,0:T(8,128)(2,1)} %param.14) | copy-start | bytes 10616836
  7.2 359.1 %all-reduce.5.cloned.1.call-start = ((), (), s32[]{:S(2)}) async-start(), calls=%async_computation | async-start | bytes 28311552 | tf_op jit(solution)/shard_map/psum | solution.py:201
  8.1 18.1 %collective-permute-start.1 = (s32[256]{0:T(256)S(1)}, s32[256]{0:T(256)S(1)}, u32[]{:S(2)}, u32[]{:S(2)}) collective-permute-start(s32[256]{0:T(256)S(1)} %bitcast.53), channel_id=1, source_target_pairs={{0,4},{4,8},{8,12},{12,16},{16,20},{20,24},{24,28},{1,5},{5,9},{9,... | collective-permute-start | bytes 3080 | tf_op jit(solution)/shard_map/ppermute | solution.py:195
  14.8 20.1 %collective-permute-start = (bf16[256,768]{1,0:T(8,128)(2,1)}, bf16[256,768]{1,0:T(8,128)(2,1)}, u32[]{:S(2)}, u32[]{:S(2)}) collective-permute-start(bf16[256,768]{1,0:T(8,128)(2,1)} %slice_bitcast_fusion), channel_id=1, source_target_pairs={{0,4},{4,8},{8,12},{12,16},{16,20},{20,24},{24,28},{1,5},{5,9},{9,... | collective-permute-start | bytes 1179656 | tf_op jit(solution)/shard_map/ppermute | solution.py:195
  31.2 3.8 copy-start.1
  31.2 6.5 %copy-start.15 = (f32[768]{0:T(1024)S(1)}, f32[768]{0:T(1024)}, u32[]{:S(2)}) copy-start(f32[768]{0:T(1024)} %convert_element_type.104) | copy-start | bytes 9220
  58.9 21.9 %copy-start.5 = (f32[512,768]{1,0:T(8,128)}, f32[512,768]{1,0:T(8,128)S(1)}, u32[]{:S(2)}) copy-start(f32[512,768]{1,0:T(8,128)S(1)} %get-tuple-element.43) | copy-start | bytes 4718596
  59.2 5.0 %copy-start.9 = (bf16[1,512,768]{2,1,0:T(8,128)(2,1)S(1)}, bf16[1,512,768]{2,1,0:T(8,128)(2,1)}, u32[]{:S(2)}) copy-start(bf16[1,512,768]{2,1,0:T(8,128)(2,1)} %param.23) | copy-start | bytes 2359300
  59.2 5.0 %copy-start.13 = (f32[512]{0:T(512)S(1)}, f32[512]{0:T(512)}, u32[]{:S(2)}) copy-start(f32[512]{0:T(512)} %compare_convert_fusion) | copy-start | bytes 6148
  59.3 10.3 %slice-start.4 = ((s8[4718592]{0:T(1024)(128)(4,1)}), s8[4194304]{0:T(1024)(128)(4,1)S(1)}, s32[]{:S(2)}) async-start(s8[4718592]{0:T(1024)(128)(4,1)} %bitcast.56), calls=%async_computation.5 | async-start | bytes 8388608
  64.2 5.3 %copy-start.21 = (f32[512,3072]{1,0:T(8,128)}, f32[512,3072]{1,0:T(8,128)S(1)}, u32[]{:S(2)}) copy-start(f32[512,3072]{1,0:T(8,128)S(1)} %fusion.26) | copy-start | bytes 18874372
  64.2 5.3 %slice-start.5 = ((s8[4718592]{0:T(1024)(128)(4,1)}), s8[524288]{0:T(1024)(128)(4,1)S(1)}, s32[]{:S(2)}) async-start(s8[4718592]{0:T(1024)(128)(4,1)} %bitcast.56), calls=%async_computation.6 | async-start | bytes 1048576
  64.3 8.3 %slice-start.2 = ((s8[4718592]{0:T(1024)(128)(4,1)}), s8[4194304]{0:T(1024)(128)(4,1)S(1)}, s32[]{:S(2)}) async-start(s8[4718592]{0:T(1024)(128)(4,1)} %bitcast.54), calls=%async_computation.3 | async-start | bytes 8388608
  81.5 3.6 copy-start.3
  113.5 5.6 %copy-start.2 = (bf16[1,512,768]{2,1,0:T(8,128)(2,1)S(1)}, bf16[1,512,768]{2,1,0:T(8,128)(2,1)}, u32[]{:S(2)}) copy-start(bf16[1,512,768]{2,1,0:T(8,128)(2,1)} %param.12) | copy-start | bytes 2359300
  123.1 7.3 %copy-start.6 = (f32[512,768]{1,0:T(8,128)S(1)}, f32[512,768]{1,0:T(8,128)}, u32[]{:S(2)}) copy-start(f32[512,768]{1,0:T(8,128)} %copy-done.5) | copy-start | bytes 4718596
  123.1 7.3 %copy-start.14 = (f32[512]{0:T(512)S(1)}, f32[512]{0:T(512)}, u32[]{:S(2)}) copy-start(f32[512]{0:T(512)} %compare_convert_fusion) | copy-start | bytes 6148
  127.6 59.5 %collective-permute-start.2 = (bf16[256,768]{1,0:T(8,128)(2,1)}, bf16[256,768]{1,0:T(8,128)(2,1)}, u32[]{:S(2)}, u32[]{:S(2)}) collective-permute-start(bf16[256,768]{1,0:T(8,128)(2,1)} %slice.67), channel_id=1, source_target_pairs={{4,0},{8,4},{12,8},{16,12},{20,16},{24,20},{28,24},{5,1},{9,5},{13... | collective-permute-start | bytes 1179656 | tf_op jit(solution)/shard_map/ppermute | solution.py:195
  130.4 8.0 %copy-start.18 = (f32[768]{0:T(1024)S(1)}, f32[768]{0:T(1024)}, u32[]{:S(2)}) copy-start(f32[768]{0:T(1024)} %get-tuple-element.27) | copy-start | bytes 9220
  130.4 9.3 %copy-start.17 = (f32[768]{0:T(1024)S(1)}, f32[768]{0:T(1024)}, u32[]{:S(2)}) copy-start(f32[768]{0:T(1024)} %get-tuple-element.31) | copy-start | bytes 9220
  130.4 56.7 %copy-start.11 = (f32[512]{0:T(512)S(1)}, f32[512]{0:T(512)}, u32[]{:S(2)}) copy-start(f32[512]{0:T(512)} %copy-done.10) | copy-start | bytes 6148
  369.3 4.5 %copy-start.7 = (bf16[768,3072]{1,0:T(8,128)(2,1)S(1)}, bf16[768,3072]{1,0:T(8,128)(2,1)}, u32[]{:S(2)}) copy-start(bf16[768,3072]{1,0:T(8,128)(2,1)} %get-tuple-element.34) | copy-start | bytes 14155780
  369.3 9.6 %slice-start = ((s8[4718592]{0:T(1024)(128)(4,1)}), s8[4194304]{0:T(1024)(128)(4,1)S(1)}, s32[]{:S(2)}) async-start(s8[4718592]{0:T(1024)(128)(4,1)} %bitcast.44), calls=%async_computation.1 | async-start | bytes 8388608
  373.9 5.1 %slice-start.1 = ((s8[4718592]{0:T(1024)(128)(4,1)}), s8[524288]{0:T(1024)(128)(4,1)S(1)}, s32[]{:S(2)}) async-start(s8[4718592]{0:T(1024)(128)(4,1)} %bitcast.44), calls=%async_computation.2 | async-start | bytes 1048576
  (8 other events, 20.5 us)
Sparse Core Ops, SparseCore 0:
  110.9 255.3 all-reduce.4
